TPU v7x, 512 devices: a whole 4x8x8 slice. The times are simulated.
512 devices in a mesh: ao: 32 (over x, z), ri: 16 (over y, core).
Axes of the slice: x: 4, y: 8, z: 8, core: 2. Of those that a mesh axis runs over, the one named last changes fastest.
Arguments:
- three_center: bfloat16 [256, 12288, 128], P('ri', 'ao'), may hold values from -0.19921875 to 0.19921875
- occ_band: bfloat16 [4096, 640], P('ao'), may hold values from -0.3125 to 0.3125
- virt_band: bfloat16 [4096, 384], P('ao'), may hold values from -0.3125 to 0.3125
- three_mask: int32 [32, 3], P('ao'), may hold values 0 or 1
- occ_mask: int32 [32, 5], P('ao'), may hold values 0 or 1
- virt_mask: int32 [32, 3], P('ao'), may hold values 0 or 1
Outputs:
- chi: float32 [256, 256], P('ri')
All inputs are finite; a program needn't handle non-finite values. No bound on the sum of `three_mask` or of `occ_mask` or of `virt_mask` on one device may be relied on, other than what follows from the above.
Results may differ from a plain program's by a relative error of at most 0.004.
Values may be sent and summed in bfloat16 or wider, within the bound.
A program may use at most 64 MiB of HBM per device.

v0:
```python
import jax
import jax.numpy as jnp
from jax import lax
from jax.sharding import PartitionSpec as P


def padded_2(value, sides, width):
    for axis, dim in sides:
        peers, length = (lax.axis_size(axis), value.shape[dim])
        up = [(i, (i + 1) % peers) for i in range(peers)]
        down = [(j, i) for i, j in up]
        last = lax.slice_in_dim(value, length - width, length, axis=dim)
        initial = lax.slice_in_dim(value, 0, width, axis=dim)
        before = lax.ppermute(last, axis, up)
        after = lax.ppermute(initial, axis, down)
        value = jnp.concatenate([before, value, after], axis=dim)
    return value


def per_device(three_center, occ_band, virt_band, three_mask, occ_mask, virt_mask):
    tile_size = occ_band.shape[0]
    local_rows = three_center.shape[0]
    live_b = (
        three_center.reshape(local_rows, 3, tile_size, tile_size)
        * three_mask[0].astype(three_center.dtype)[None, :, None, None]
    )
    live_b = live_b.reshape(local_rows, 3 * tile_size, tile_size)
    live_occ = occ_band * jnp.repeat(occ_mask[0].astype(occ_band.dtype), tile_size)[None, :]
    live_virt = virt_band * jnp.repeat(virt_mask[0].astype(virt_band.dtype), tile_size)[None, :]
    occ_rows = padded_2(live_occ, (("ao", 0),), tile_size)
    blank = jnp.zeros((tile_size, tile_size), occ_band.dtype)
    green_block = jnp.concatenate(
        [
            jnp.concatenate([occ_rows[0:tile_size, tile_size:], blank], 1),
            occ_rows[tile_size : 2 * tile_size],
            jnp.concatenate([blank, occ_rows[2 * tile_size :, : 4 * tile_size]], 1),
        ],
        0,
    )
    m_local = jnp.einsum(
        "ml,pmn->pln", green_block, live_b, preferred_element_type=jnp.float32
    ).astype(jnp.bfloat16)
    padded = padded_2(m_local, (("ao", 2),), tile_size)
    needed = jnp.concatenate(
        [
            padded[:, 2 * tile_size : 5 * tile_size, 0:tile_size],
            padded[:, tile_size : 4 * tile_size, tile_size : 2 * tile_size],
            padded[:, 0 : 3 * tile_size, 2 * tile_size : 3 * tile_size],
        ],
        2,
    )
    product = jnp.einsum(
        "plv,sv->pls", needed, live_virt, preferred_element_type=jnp.float32
    ).astype(jnp.bfloat16)
    product_flat = product.reshape(local_rows, 3 * tile_size * tile_size)
    b_flat = live_b.reshape(local_rows, 3 * tile_size * tile_size)
    product_all, b_all = (
        lax.all_to_all(product_flat, "ri", split_axis=1, concat_axis=0, tiled=True),
        lax.all_to_all(b_flat, "ri", split_axis=1, concat_axis=0, tiled=True),
    )
    partial_chi = lax.dot_general(
        product_all, b_all, (((1,), (1,)), ((), ())), preferred_element_type=jnp.float32
    )
    row_panel = lax.psum_scatter(partial_chi, "ri", scatter_dimension=0, tiled=True)
    summed = lax.psum(row_panel, "ao")
    return -summed


def solution(mesh):
    placed = (
        P("ri", "ao", None),
        P("ao", None),
        P("ao", None),
        P("ao", None),
        P("ao", None),
        P("ao", None),
    )
    return jax.shard_map(
        per_device, mesh=mesh, in_specs=placed, out_specs=P("ri", None), check_vma=False
    )
```

profile of v0, /device:TPU:32, one launch (start us, length us, event | category | flops | bytes accessed | tf_op | source)
XLA Modules:
  0.0 353.9 jit_solution(3540133267525671056)
XLA Ops:
  6.5 0.7 convert_bitcast_fusion.2
  7.2 0.1 broadcast_bitcast_fusion
  7.3 0.9 broadcast_multiply_fusion.1
  8.2 4.3 %collective-permute-start = (bf16[128,640]{1,0:T(8,128)(2,1)S(1)}, bf16[128,640]{1,0:T(8,128)(2,1)}, u32[]{:S(2)}, u32[]{:S(2)}) collective-permute-start(bf16[128,640]{1,0:T(8,128)(2,1)S(1)} %broadcast_multiply_fusion.1), channel_id=1, source_target_pairs={{0,16},{16,32},{32,48},{48,64},{64,80},{80,96},{96,112},{112,128},... | collective-permute-start | bytes 491528 | tf_op jit(solution)/shard_map/ppermute | solution.py:14
  12.5 10.8 %collective-permute-start.1 = (bf16[128,640]{1,0:T(8,128)(2,1)S(1)}, bf16[128,640]{1,0:T(8,128)(2,1)}, u32[]{:S(2)}, u32[]{:S(2)}) collective-permute-start(bf16[128,640]{1,0:T(8,128)(2,1)S(1)} %broadcast_multiply_fusion.1), channel_id=1, source_target_pairs={{16,0},{32,16},{48,32},{64,48},{80,64},{96,80},{112,96},{128,112},... | collective-permute-start | bytes 491528 | tf_op jit(solution)/shard_map/ppermute | solution.py:15
  23.3 0.7 convert_bitcast_fusion.3
  23.9 0.1 mul.53
  24.1 2.7 reshape.31
  26.8 0.1 broadcast_bitcast_fusion.2
  26.9 0.9 slice.20
  27.8 0.9 slice.21
  28.7 3.3 convert_bitcast_fusion
  32.0 1.9 collective-permute-start.2
  34.0 7.2 %collective-permute-start.3 = (bf16[16,640,128]{1,2,0:T(8,128)(2,1)}, bf16[16,640,128]{1,2,0:T(8,128)(2,1)}, u32[]{:S(2)}, u32[]{:S(2)}) collective-permute-start(bf16[16,640,128]{1,2,0:T(8,128)(2,1)} %convert_bitcast_fusion), channel_id=1, source_target_pairs={{16,0},{32,16},{48,32},{64,48},{80,64},{96,80},{112,96},{128,112},... | collective-permute-start | bytes 7864328 | tf_op jit(solution)/shard_map/ppermute | solution.py:15
  41.2 0.1 broadcast_multiply_fusion
  41.3 2.0 copy.19
  43.4 7.4 %all-to-all-start.1 = ((bf16[16,16,3072]{2,0,1:T(8,128)(2,1)}), bf16[16,16,3072]{2,0,1:T(8,128)(2,1)}, u32[]{:S(2)}, u32[]{:S(2)}) async-start(bf16[16,16,3072]{2,0,1:T(8,128)(2,1)} %copy.19), calls=%async_computation.1 | async-start | bytes 3145728 | tf_op jit(solution)/shard_map/all_to_all | solution.py:59
  50.7 0.0 reduce-scatter.2.cloned.1.call-start
  50.8 0.1 broadcast_bitcast_fusion.1
  50.9 1.6 slice.23
  52.5 43.4 %collective-permute-done.2 = bf16[16,640,128]{1,2,0:T(8,128)(2,1)} collective-permute-done((bf16[16,640,128]{1,2,0:T(8,128)(2,1)}, bf16[16,640,128]{1,2,0:T(8,128)(2,1)}, u32[]{:S(2)}, u32[]{:S(2)}) %collective-permute-start.2) | collective-permute-done | bytes 2621472 | tf_op jit(solution)/shard_map/ppermute | solution.py:14
  95.9 1.6 slice.22
  97.5 1.6 slice.24
  99.2 1.7 fusion.6
  100.8 0.7 all_to_all.26
  101.5 0.9 copy.18
  102.4 42.5 %all_to_all.35 = bf16[16,16,3072]{2,0,1:T(8,128)(2,1)S(1)} all-to-all(bf16[16,16,3072]{2,0,1:T(8,128)(2,1)S(1)} %copy.18), channel_id=1, replica_groups=mesh['ao'=32,'ri'=16] {'ri'}, dimensions={1} | all-to-all | bytes 3145728 | tf_op jit(solution)/shard_map/all_to_all | solution.py:58
  144.9 2.7 fusion.32
  147.6 0.0 reduce-scatter.2.cloned.1.call-update
  147.6 55.1 %reduce-scatter.2.cloned.1.call-done = f32[16,256]{1,0:T(8,128)} async-done(((f32[256,256]{1,0:T(8,128)}), f32[16,256]{1,0:T(8,128)}) %reduce-scatter.2.cloned.1.call-update) | async-done | bytes 16400 | tf_op jit(solution)/shard_map/reduce_scatter | solution.py:64
  202.8 143.7 %psum.7 = f32[16,256]{1,0:T(8,128)S(1)} all-reduce(f32[16,256]{1,0:T(8,128)} %reduce-scatter.2.cloned.1.call-done), channel_id=1, replica_groups=mesh['ao'=32,'ri'=16] {'ao'}, use_global_device_ids=true, to_apply=%region_1.0 | all-reduce | flops 4096 | bytes 32768 | tf_op jit(solution)/shard_map/psum | solution.py:65
  346.5 0.6 neg.3
  (12 shorter events, 0.1 us)
Async XLA Ops:
  8.2 18.7 %collective-permute-start = (bf16[128,640]{1,0:T(8,128)(2,1)S(1)}, bf16[128,640]{1,0:T(8,128)(2,1)}, u32[]{:S(2)}, u32[]{:S(2)}) collective-permute-start(bf16[128,640]{1,0:T(8,128)(2,1)S(1)} %broadcast_multiply_fusion.1), channel_id=1, source_target_pairs={{0,16},{16,32},{32,48},{48,64},{64,80},{80,96},{96,112},{112,128},... | collective-permute-start | bytes 491528 | tf_op jit(solution)/shard_map/ppermute | solution.py:14
  12.5 15.3 %collective-permute-start.1 = (bf16[128,640]{1,0:T(8,128)(2,1)S(1)}, bf16[128,640]{1,0:T(8,128)(2,1)}, u32[]{:S(2)}, u32[]{:S(2)}) collective-permute-start(bf16[128,640]{1,0:T(8,128)(2,1)S(1)} %broadcast_multiply_fusion.1), channel_id=1, source_target_pairs={{16,0},{32,16},{48,32},{64,48},{80,64},{96,80},{112,96},{128,112},... | collective-permute-start | bytes 491528 | tf_op jit(solution)/shard_map/ppermute | solution.py:15
  24.1 4.6 %copy-start = (bf16[16,384,128]{2,1,0:T(8,128)(2,1)S(1)}, bf16[16,384,128]{2,1,0:T(8,128)(2,1)}, u32[]{:S(2)}) copy-start(bf16[16,384,128]{2,1,0:T(8,128)(2,1)} %param.6) | copy-start | bytes 4718596
  32.0 63.8 %collective-permute-start.2 = (bf16[16,640,128]{1,2,0:T(8,128)(2,1)}, bf16[16,640,128]{1,2,0:T(8,128)(2,1)}, u32[]{:S(2)}, u32[]{:S(2)}) collective-permute-start(bf16[16,640,128]{1,2,0:T(8,128)(2,1)} %convert_bitcast_fusion), channel_id=1, source_target_pairs={{0,16},{16,32},{32,48},{48,64},{64,80},{80,96},{96,112},{112,128},... | collective-permute-start | bytes 7864328 | tf_op jit(solution)/shard_map/ppermute | solution.py:14
  34.0 63.5 %collective-permute-start.3 = (bf16[16,640,128]{1,2,0:T(8,128)(2,1)}, bf16[16,640,128]{1,2,0:T(8,128)(2,1)}, u32[]{:S(2)}, u32[]{:S(2)}) collective-permute-start(bf16[16,640,128]{1,2,0:T(8,128)(2,1)} %convert_bitcast_fusion), channel_id=1, source_target_pairs={{16,0},{32,16},{48,32},{64,48},{80,64},{96,80},{112,96},{128,112},... | collective-permute-start | bytes 7864328 | tf_op jit(solution)/shard_map/ppermute | solution.py:15
  43.4 7.4 %copy-start.2 = (s32[1,3]{1,0:T(1,128)S(1)}, s32[1,3]{1,0:T(1,128)}, u32[]{:S(2)}) copy-start(s32[1,3]{1,0:T(1,128)} %param.11) | copy-start | bytes 40
  43.4 59.0 %all-to-all-start.1 = ((bf16[16,16,3072]{2,0,1:T(8,128)(2,1)}), bf16[16,16,3072]{2,0,1:T(8,128)(2,1)}, u32[]{:S(2)}, u32[]{:S(2)}) async-start(bf16[16,16,3072]{2,0,1:T(8,128)(2,1)} %copy.19), calls=%async_computation.1 | async-start | bytes 3145728 | tf_op jit(solution)/shard_map/all_to_all | solution.py:59
  50.7 152.0 %reduce-scatter.2.cloned.1.call-start = ((), (), s32[]{:S(2)}) async-start(), calls=%async_computation.3 | async-start | bytes 278528 | tf_op jit(solution)/shard_map/reduce_scatter | solution.py:64
  97.5 1.7 copy-start.1
Sparse Core Ops, SparseCore 0:
  147.8 54.9 reduce-scatter.1
where the time goes:
time: 354 us
  blocking collectives  186 us (53%)
  waiting for transfers between devices  98.6 us (28%)
  starting transfers between devices  31.6 us (9%)
  between operations  13.6 us (4%)
  local copies, waits for them, and re-layouts  13.3 us (4%)
  matrix products  7.72 us (2%)
    psum x1, blocking collectives, per_device(): summed = lax.psum(row_panel, 'ao')  144 us
    reduce_scatter x1, waiting for transfers between devices, per_device(): lax.psum_scatter(partial_chi, 'ri', scatter_dimension=0, tiled=True)  55.1 us
    ppermute x2, waiting for transfers between devices, padded_2(): before = lax.ppermute(last, axis, up)  43.4 us
    all_to_all x1, blocking collectives, per_device(): lax.all_to_all(product_flat, 'ri', split_axis=1, concat_axis=0, tiled=True)  42.5 us
    ppermute x2, starting transfers between devices, padded_2(): after = lax.ppermute(initial, axis, down)  18 us
    all_to_all x1, starting transfers between devices, per_device(): lax.all_to_all(b_flat, 'ri', split_axis=1, concat_axis=0, tiled=True)  7.36 us
  transfers between devices with their start and end apart: 6, of which 2 were waited for; matrix products, arithmetic and copies ran while one was open for 4% of the time, Pallas kernels for 0%

commit v1 on v0

--- a/solution.py
+++ b/solution.py
@@ -55,7 +55,12 @@
     product_flat = product.reshape(local_rows, 3 * tile_size * tile_size)
     b_flat = live_b.reshape(local_rows, 3 * tile_size * tile_size)
     product_all, b_all = (
-        lax.all_to_all(product_flat, "ri", split_axis=1, concat_axis=0, tiled=True),
+        jnp.concatenate(
+            lax.all_to_all(
+                jnp.stack(jnp.split(product_flat, lax.axis_size("ri"), axis=1)), "ri", 0, 0
+            ),
+            axis=0,
+        ),
         lax.all_to_all(b_flat, "ri", split_axis=1, concat_axis=0, tiled=True),
     )
     partial_chi = lax.dot_general(

time: 354 us -> 352 us (level)
  local copies, waits for them, and re-layouts: 13.3 us -> 9.16 us
  transfers between devices with their start and end apart: 6 -> 6, of which waited for: 2 -> 4; matrix products, arithmetic and copies ran while one was open for 4% -> 3% of each run, Pallas kernels for 0% -> 0%
where the time goes in v1:
time: 352 us
  blocking collectives  186 us (53%)
  waiting for transfers between devices  100 us (28%)
  starting transfers between devices  32.1 us (9%)
  between operations  13.7 us (4%)
  local copies, waits for them, and re-layouts  9.16 us (3%)
  matrix products  7.85 us (2%)
    psum x1, blocking collectives, per_device(): summed = lax.psum(row_panel, 'ao')  144 us
    reduce_scatter x1, waiting for transfers between devices, per_device(): lax.psum_scatter(partial_chi, 'ri', scatter_dimension=0, tiled=True)  55.2 us
    ppermute x2, waiting for transfers between devices, padded_2(): before = lax.ppermute(last, axis, up)  43.7 us
    all_to_all x1, blocking collectives, per_device(): lax.all_to_all(jnp.stack(jnp.split(product_flat, lax.axis_size('ri'), axi...  42.5 us
    ppermute x2, starting transfers between devices, padded_2(): after = lax.ppermute(initial, axis, down)  18.5 us
    all_to_all x1, starting transfers between devices, per_device(): lax.all_to_all(b_flat, 'ri', split_axis=1, concat_axis=0, tiled=True)  7.36 us
  transfers between devices with their start and end apart: 6, of which 4 were waited for; matrix products, arithmetic and copies ran while one was open for 3% of the time, Pallas kernels for 0%

profile of v1, /device:TPU:32, one launch (start us, length us, event | category | flops | bytes accessed | tf_op | source)
XLA Modules:
  0.0 352.0 jit_solution(10024042779054979978)
XLA Ops:
  6.5 0.7 convert_bitcast_fusion.2
  7.2 0.1 broadcast_bitcast_fusion
  7.3 0.9 broadcast_multiply_fusion.1
  8.2 4.3 %collective-permute-start = (bf16[128,640]{1,0:T(8,128)(2,1)S(1)}, bf16[128,640]{1,0:T(8,128)(2,1)S(1)}, u32[]{:S(2)}, u32[]{:S(2)}) collective-permute-start(bf16[128,640]{1,0:T(8,128)(2,1)S(1)} %broadcast_multiply_fusion.1), channel_id=1, source_target_pairs={{0,16},{16,32},{32,48},{48,64},{64,80},{80,96},{96,112},{112,128},... | collective-permute-start | bytes 491528 | tf_op jit(solution)/shard_map/ppermute | solution.py:14
  12.5 10.8 %collective-permute-start.1 = (bf16[128,640]{1,0:T(8,128)(2,1)S(1)}, bf16[128,640]{1,0:T(8,128)(2,1)S(1)}, u32[]{:S(2)}, u32[]{:S(2)}) collective-permute-start(bf16[128,640]{1,0:T(8,128)(2,1)S(1)} %broadcast_multiply_fusion.1), channel_id=1, source_target_pairs={{16,0},{32,16},{48,32},{64,48},{80,64},{96,80},{112,96},{128,112},... | collective-permute-start | bytes 491528 | tf_op jit(solution)/shard_map/ppermute | solution.py:15
  23.3 0.7 convert_bitcast_fusion.3
  23.9 0.1 broadcast_bitcast_fusion.2
  24.0 1.5 collective-permute-done
  25.6 1.2 collective-permute-done.1
  26.7 0.0 copy-start
  26.7 4.9 %convert_bitcast_fusion = bf16[16,640,128]{1,2,0:T(8,128)(2,1)} fusion(bf16[16,384,128]{2,1,0:T(8,128)(2,1)} %param.6, bf16[384]{0:T(512)(128)(2,1)S(1)} %broadcast_bitcast_fusion.2, bf16[128,512]{1,0:T(8,128)(2,1)S(1)} %slice.21, bf16[128,512]{1,0:T(8,128)(2,1)S(1)} %slice.20, bf16[128,640]{1,0:T(8,128)(2,1)S(1)} %broadcast_multiply_fusion.1), kind=kOutput, calls=%fused_computation.6 | convolution fusion | flops 1011187712 | bytes 4621056 | tf_op jit(solution)/shard_map/ml,pmn->pln/dot_general | solution.py:40
  31.6 1.9 collective-permute-start.2
  33.5 7.7 %collective-permute-start.3 = (bf16[16,640,128]{1,2,0:T(8,128)(2,1)}, bf16[16,640,128]{1,2,0:T(8,128)(2,1)}, u32[]{:S(2)}, u32[]{:S(2)}) collective-permute-start(bf16[16,640,128]{1,2,0:T(8,128)(2,1)} %convert_bitcast_fusion), channel_id=1, source_target_pairs={{16,0},{32,16},{48,32},{64,48},{80,64},{96,80},{112,96},{128,112},... | collective-permute-start | bytes 7864328 | tf_op jit(solution)/shard_map/ppermute | solution.py:15
  41.2 0.7 reshape.34
  42.0 0.1 mul.53
  42.1 0.1 broadcast_multiply_fusion
  42.2 2.1 copy.16
  44.3 7.4 %all-to-all-start.1 = ((bf16[16,16,3072]{2,0,1:T(8,128)(2,1)}), bf16[16,16,3072]{2,0,1:T(8,128)(2,1)S(1)}, u32[]{:S(2)}, u32[]{:S(2)}) async-start(bf16[16,16,3072]{2,0,1:T(8,128)(2,1)} %copy.16), calls=%async_computation.1 | async-start | bytes 3145728 | tf_op jit(solution)/shard_map/all_to_all | solution.py:64
  51.7 0.0 reduce-scatter.2.cloned.1.call-start
  51.8 0.1 broadcast_bitcast_fusion.1
  51.8 1.6 slice.23
  53.4 42.2 %collective-permute-done.2 = bf16[16,640,128]{1,2,0:T(8,128)(2,1)} collective-permute-done((bf16[16,640,128]{1,2,0:T(8,128)(2,1)}, bf16[16,640,128]{1,2,0:T(8,128)(2,1)}, u32[]{:S(2)}, u32[]{:S(2)}) %collective-permute-start.2) | collective-permute-done | bytes 2621472 | tf_op jit(solution)/shard_map/ppermute | solution.py:14
  95.6 1.6 slice.22
  97.2 1.6 slice.24
  98.9 1.7 fusion.6
  100.5 1.0 copy.21
  101.8 42.5 %all_to_all.21 = bf16[16,16,3072]{2,1,0:T(8,128)(2,1)S(1)} all-to-all(bf16[16,16,3072]{2,1,0:T(8,128)(2,1)S(1)} %fusion.24), channel_id=1, replica_groups=mesh['ao'=32,'ri'=16] {'ri'}, dimensions={0} | all-to-all | bytes 3145728 | tf_op jit(solution)/shard_map/all_to_all | solution.py:59
  144.3 1.3 fusion.48
  145.6 0.0 reduce-scatter.2.cloned.1.call-update
  145.7 55.2 %reduce-scatter.2.cloned.1.call-done = f32[16,256]{1,0:T(8,128)} async-done(((f32[256,256]{1,0:T(8,128)}), f32[16,256]{1,0:T(8,128)}) %reduce-scatter.2.cloned.1.call-update) | async-done | bytes 16400 | tf_op jit(solution)/shard_map/reduce_scatter | solution.py:69
  200.8 143.7 %psum.7 = f32[16,256]{1,0:T(8,128)S(1)} all-reduce(f32[16,256]{1,0:T(8,128)} %reduce-scatter.2.cloned.1.call-done), channel_id=1, replica_groups=mesh['ao'=32,'ri'=16] {'ao'}, use_global_device_ids=true, to_apply=%region_1.0 | all-reduce | flops 4096 | bytes 32768 | tf_op jit(solution)/shard_map/psum | solution.py:70
  344.5 0.6 neg.3
  (27 shorter events, 0.2 us)
Async XLA Ops:
  8.2 17.3 %collective-permute-start = (bf16[128,640]{1,0:T(8,128)(2,1)S(1)}, bf16[128,640]{1,0:T(8,128)(2,1)S(1)}, u32[]{:S(2)}, u32[]{:S(2)}) collective-permute-start(bf16[128,640]{1,0:T(8,128)(2,1)S(1)} %broadcast_multiply_fusion.1), channel_id=1, source_target_pairs={{0,16},{16,32},{32,48},{48,64},{64,80},{80,96},{96,112},{112,128},... | collective-permute-start | bytes 491528 | tf_op jit(solution)/shard_map/ppermute | solution.py:14
  12.5 14.2 %collective-permute-start.1 = (bf16[128,640]{1,0:T(8,128)(2,1)S(1)}, bf16[128,640]{1,0:T(8,128)(2,1)S(1)}, u32[]{:S(2)}, u32[]{:S(2)}) collective-permute-start(bf16[128,640]{1,0:T(8,128)(2,1)S(1)} %broadcast_multiply_fusion.1), channel_id=1, source_target_pairs={{16,0},{32,16},{48,32},{64,48},{80,64},{96,80},{112,96},{128,112},... | collective-permute-start | bytes 491528 | tf_op jit(solution)/shard_map/ppermute | solution.py:15
  26.7 14.5 %copy-start = (bf16[16,384,128]{2,1,0:T(8,128)(2,1)S(1)}, bf16[16,384,128]{2,1,0:T(8,128)(2,1)}, u32[]{:S(2)}) copy-start(bf16[16,384,128]{2,1,0:T(8,128)(2,1)} %param.6) | copy-start | bytes 4718596
  31.6 64.0 %collective-permute-start.2 = (bf16[16,640,128]{1,2,0:T(8,128)(2,1)}, bf16[16,640,128]{1,2,0:T(8,128)(2,1)}, u32[]{:S(2)}, u32[]{:S(2)}) collective-permute-start(bf16[16,640,128]{1,2,0:T(8,128)(2,1)} %convert_bitcast_fusion), channel_id=1, source_target_pairs={{0,16},{16,32},{32,48},{48,64},{64,80},{80,96},{96,112},{112,128},... | collective-permute-start | bytes 7864328 | tf_op jit(solution)/shard_map/ppermute | solution.py:14
  33.5 63.7 %collective-permute-start.3 = (bf16[16,640,128]{1,2,0:T(8,128)(2,1)}, bf16[16,640,128]{1,2,0:T(8,128)(2,1)}, u32[]{:S(2)}, u32[]{:S(2)}) collective-permute-start(bf16[16,640,128]{1,2,0:T(8,128)(2,1)} %convert_bitcast_fusion), channel_id=1, source_target_pairs={{16,0},{32,16},{48,32},{64,48},{80,64},{96,80},{112,96},{128,112},... | collective-permute-start | bytes 7864328 | tf_op jit(solution)/shard_map/ppermute | solution.py:15
  44.3 7.4 %copy-start.2 = (s32[1,3]{1,0:T(1,128)S(1)}, s32[1,3]{1,0:T(1,128)}, u32[]{:S(2)}) copy-start(s32[1,3]{1,0:T(1,128)} %param.11) | copy-start | bytes 40
  44.3 57.5 %all-to-all-start.1 = ((bf16[16,16,3072]{2,0,1:T(8,128)(2,1)}), bf16[16,16,3072]{2,0,1:T(8,128)(2,1)S(1)}, u32[]{:S(2)}, u32[]{:S(2)}) async-start(bf16[16,16,3072]{2,0,1:T(8,128)(2,1)} %copy.16), calls=%async_computation.1 | async-start | bytes 3145728 | tf_op jit(solution)/shard_map/all_to_all | solution.py:64
  51.7 149.1 %reduce-scatter.2.cloned.1.call-start = ((), (), s32[]{:S(2)}) async-start(), calls=%async_computation.3 | async-start | bytes 278528 | tf_op jit(solution)/shard_map/reduce_scatter | solution.py:69
  97.2 1.7 copy-start.1
Sparse Core Ops, SparseCore 0:
  145.8 54.9 reduce-scatter.1
